TPU v7x, 32 devices: a whole 2x2x4 slice. The times are simulated.
32 devices in a mesh: wide: 16 (over z, x, core), narrow: 2 (over y).
Axes of the slice: x: 2, y: 2, z: 4, core: 2. Of those that a mesh axis runs over, the one named last changes fastest.
Arguments:
- activations: float32 [1024, 17408], P('wide', 'narrow'), may hold values from -6 to 6
- act_basis: float32 [17408, 17408], P('narrow', 'wide'), may hold values from -0.046875 to 0.046875
- grads: float32 [1024, 5120], P(None, 'wide'), may hold values from -0.3 to 0.3
- grad_basis: float32 [5120, 5120], P('wide', 'narrow'), may hold values from -0.078125 to 0.078125
- seq_ids: int32 [1024], replicated, may hold values from 0 to 3, never falling along the last dimension, each value on 1 to 512 neighbouring positions
Outputs:
- eigenvalues: float32 [17408, 5120], P('wide', 'narrow')
Inputs may be any that keep to these rules, and one draw needn't show every extreme that they name: `seq_ids`: never falling along the rows; every sequence has at least one row and at most 512 rows, and one sequence has exactly 512.
All inputs are finite; a program needn't handle non-finite values.
Results may differ from a plain program's by a relative error of at most 0.0003.
Values sent between devices are 32-bit elements; how exact they have to be, the bound alone decides.
A program may use at most 192 MiB of HBM per device.

v0:
```python
import jax
import jax.numpy as jnp
from jax import lax
from jax.sharding import PartitionSpec as P

SEQS = 4
SEQ_MOST = 512


def seq_window(rotated_acts, rotated_grads, seq_ids, seq_label):
    token_rows = rotated_grads.shape[0]
    first_row = jnp.sum((seq_ids < seq_label).astype(jnp.int32))
    window_start = jnp.minimum(first_row, token_rows - SEQ_MOST)
    acts_window = lax.dynamic_slice_in_dim(rotated_acts, window_start, SEQ_MOST, 0)
    grads_window = lax.dynamic_slice_in_dim(rotated_grads, window_start, SEQ_MOST, 0)
    ids_window = lax.dynamic_slice_in_dim(seq_ids, window_start, SEQ_MOST, 0)
    seq_mask = (ids_window == seq_label).astype(jnp.float32)[:, None]
    return (acts_window, grads_window * seq_mask)


def per_device(activations, act_basis, grads, grad_basis, seq_ids):
    highest = lax.Precision.HIGHEST
    partial_acts = jnp.dot(
        lax.all_gather(activations, "wide", axis=0, tiled=True),
        act_basis,
        precision=highest,
        preferred_element_type=jnp.float32,
    )
    rotated_acts = lax.psum(partial_acts, "narrow")
    partial_grads = jnp.dot(
        grads, grad_basis, precision=highest, preferred_element_type=jnp.float32
    )
    rotated_grads = lax.psum(partial_grads, "wide")
    out_cols = rotated_grads.shape[1]
    running = jnp.zeros((rotated_acts.shape[1], out_cols), jnp.float32)
    for seq_label in range(SEQS):
        acts_window, grads_window = seq_window(rotated_acts, rotated_grads, seq_ids, seq_label)
        moment = jnp.dot(
            acts_window.T, grads_window, precision=highest, preferred_element_type=jnp.float32
        )
        running = running + moment * moment
    return running / jnp.float32(SEQS)


def solution(mesh):
    in_specs = (P("wide", "narrow"), P("narrow", "wide"), P(None, "wide"), P("wide", "narrow"), P())
    out_specs = P("wide", "narrow")
    return jax.shard_map(
        per_device, mesh=mesh, in_specs=in_specs, out_specs=out_specs, check_vma=False
    )
```

profile of v0, /device:TPU:0, one launch (start us, length us, event | category | flops | bytes accessed | tf_op | source)
XLA Modules:
  0.0 607.1 jit_solution(9304746979321440647)
XLA Ops:
  6.5 0.0 copy-start
  6.5 0.0 all-gather.2.cloned.1.call-start
  6.5 0.7 all-gather.2.cloned.1.call-update
  7.3 0.0 all-reduce.5.cloned.1.call-start
  7.3 1.2 copy-done
  8.5 20.3 %fusion.29 = f32[1024,2560]{1,0:T(8,128)} fusion(f32[1024,320]{0,1:T(8,128)} %param.7, f32[320,2560]{1,0:T(8,128)S(1)} %copy-done), kind=kOutput, calls=%fused_computation.41 | convolution fusion | flops 10066329600 | bytes 15073280 | tf_op jit(solution)/shard_map/dot_general | solution.py:30
  28.8 0.0 all-reduce.5.cloned.1.call-update
  28.8 0.0 copy-start.3
  28.8 0.6 all-reduce.3.cloned.1.call-start
  29.4 160.2 %all-gather.2.cloned.1.call-done = f32[1024,8704]{1,0:T(8,128)} async-done(((f32[64,8704]{1,0:T(8,128)}), f32[1024,8704]{1,0:T(8,128)}) %all-gather.2.cloned.1.call-update) | async-done | bytes 35651600 | tf_op jit(solution)/shard_map/all_gather | solution.py:24
  189.6 127.6 %fusion.28 = f32[1024,1088]{0,1:T(8,128)} fusion(f32[1024,8704]{1,0:T(8,128)} %all-gather.2.cloned.1.call-done, f32[8704,1088]{0,1:T(8,128)} %param.6), kind=kOutput, calls=%fused_computation.40 | convolution fusion | flops 116366770176 | bytes 77987840 | tf_op jit(solution)/shard_map/dot_general | solution.py:23
  317.2 0.0 all-reduce.3.cloned.1.call-update
  317.3 0.0 copy-done.3
  317.3 0.7 convert_reduce_fusion
  320.5 0.1 fusion.27
  320.6 73.7 %all-reduce.5.cloned.1.call-done = f32[1024,2560]{1,0:T(8,128)} async-done(((f32[1024,2560]{1,0:T(8,128)}), f32[1024,2560]{1,0:T(8,128)}) %all-reduce.5.cloned.1.call-update) | async-done | bytes 10485776 | tf_op jit(solution)/shard_map/psum | solution.py:33
  394.3 116.0 %all-reduce.3.cloned.1.call-done = f32[1024,1088]{0,1:T(8,128)} async-done(((f32[1024,1088]{0,1:T(8,128)}), f32[1024,1088]{0,1:T(8,128)}) %all-reduce.3.cloned.1.call-update) | async-done | bytes 4456464 | tf_op jit(solution)/shard_map/psum | solution.py:29
  510.4 0.0 copy-start.2
  510.4 22.4 %convolution_multiply_fusion.2 = f32[1088,2560]{1,0:T(8,128)S(1)} fusion(f32[1024,2560]{1,0:T(8,128)} %all-reduce.5.cloned.1.call-done, s32[]{:T(128)S(6)} %select_n.9, f32[512]{0:T(512)S(1)} %get-tuple-element.12, f32[1024,1088]{0,1:T(8,128)} %all-reduce.3.cloned.1.call-done), kind=kOutput, calls=%fused_computation.2 | convolution fusion | flops 17116856320 | bytes 18615296 | tf_op jit(solution)/shard_map/dot_general | solution.py:38
  532.7 0.0 copy-done.2
  532.7 21.9 %fusion = f32[1088,2560]{1,0:T(8,128)S(1)} fusion(f32[1088,2560]{1,0:T(8,128)S(1)} %convolution_multiply_fusion.2, f32[1024,2560]{1,0:T(8,128)} %all-reduce.5.cloned.1.call-done, s32[]{:T(128)S(6)} %select_n.8, f32[512]{0:T(512)S(1)} %get-tuple-element.11, f32[1024,1088]{0,1:T(8,128)S(1)} %copy-done.2), kind=kOutput, calls=%fused_computation.4 | convolution fusion | flops 17119641600 | bytes 29756416 | tf_op jit(solution)/shard_map/dot_general | solution.py:38
  554.7 21.9 %fusion.1 = f32[1088,2560]{1,0:T(8,128)S(1)} fusion(f32[1088,2560]{1,0:T(8,128)S(1)} %fusion, f32[1024,2560]{1,0:T(8,128)} %all-reduce.5.cloned.1.call-done, s32[]{:T(128)S(6)} %select_n.10, f32[512]{0:T(512)S(1)} %get-tuple-element.10, f32[1024,1088]{0,1:T(8,128)S(1)} %copy-done.2), kind=kOutput, calls=%fused_computation.5 | convolution fusion | flops 17119641600 | bytes 29756416 | tf_op jit(solution)/shard_map/dot_general | solution.py:38
  576.6 0.0 copy-start.1
  576.6 23.4 %fusion.3 = f32[1088,2560]{1,0:T(8,128)} fusion(f32[1088,2560]{1,0:T(8,128)S(1)} %fusion.1, f32[1024,2560]{1,0:T(8,128)} %all-reduce.5.cloned.1.call-done, s32[]{:T(128)S(6)} %select_n.11, f32[512]{0:T(512)S(1)} %get-tuple-element.9, f32[1024,1088]{0,1:T(8,128)S(1)} %copy-done.2), kind=kOutput, calls=%fused_computation.7 | convolution fusion | flops 17122426880 | bytes 29756416 | tf_op jit(solution)/shard_map/dot_general | solution.py:38
  600.0 0.0 copy-done.1
Async XLA Ops:
  6.5 1.9 copy-start
  6.5 183.1 %all-gather.2.cloned.1.call-start = ((), (), s32[]{:S(2)}) async-start(), calls=%async_computation | async-start | bytes 37879808 | tf_op jit(solution)/shard_map/all_gather | solution.py:24
  7.3 387.1 %all-reduce.5.cloned.1.call-start = ((), (), s32[]{:S(2)}) async-start(), calls=%async_computation.2 | async-start | bytes 20971520 | tf_op jit(solution)/shard_map/psum | solution.py:33
  28.8 288.4 %copy-start.3 = (s32[1024]{0:T(1024)S(1)}, s32[1024]{0:T(1024)}, u32[]{:S(2)}) copy-start(s32[1024]{0:T(1024)} %param.9) | copy-start | bytes 12292
  28.8 481.5 %all-reduce.3.cloned.1.call-start = ((), (), s32[]{:S(2)}) async-start(), calls=%async_computation.1 | async-start | bytes 8912896 | tf_op jit(solution)/shard_map/psum | solution.py:29
  510.4 22.4 %copy-start.2 = (f32[1024,1088]{0,1:T(8,128)S(1)}, f32[1024,1088]{0,1:T(8,128)}, u32[]{:S(2)}) copy-start(f32[1024,1088]{0,1:T(8,128)} %all-reduce.3.cloned.1.call-done) | copy-start | bytes 13369348
  576.6 23.4 %copy-start.1 = (f32[320,2560]{1,0:T(8,128)S(1)}, f32[320,2560]{1,0:T(8,128)}, u32[]{:S(2)}) copy-start(f32[320,2560]{1,0:T(8,128)} %param.8) | copy-start | bytes 9830404
Sparse Core Ops, SparseCore 0:
  8.9 180.6 all-gather.1
  193.4 200.9 all-reduce.4
  396.8 113.5 all-reduce.2
where the time goes:
time: 614 us; the launch traced here: 607 us
  waiting for transfers between devices  351 us (57%)
  matrix products  238 us (39%)
  between operations  16.2 us (3%)
    all_gather x1, waiting for transfers between devices, per_device(): lax.all_gather(activations, 'wide', axis=0, tiled=True)  160 us
    dot_general x1, matrix products, per_device(): jnp.dot(lax.all_gather(activations, 'wide', axis=0, tiled=True), act_basi...  128 us
    psum x1, waiting for transfers between devices, per_device(): rotated_acts = lax.psum(partial_acts, 'narrow')  116 us
    dot_general x4, matrix products, per_device(): jnp.dot(acts_window.T, grads_window, precision=highest, preferred_element...  89.6 us
    psum x1, waiting for transfers between devices, per_device(): rotated_grads = lax.psum(partial_grads, 'wide')  73.7 us
    dot_general x1, matrix products, per_device(): jnp.dot(grads, grad_basis, precision=highest, preferred_element_type=jnp....  20.3 us
  transfers between devices with their start and end apart: 3, of which 3 were waited for; matrix products, arithmetic and copies ran while one was open for 25% of the time, Pallas kernels for 0%

commit v1 on v0

--- a/solution.py
+++ b/solution.py
@@ -30,7 +30,13 @@
     partial_grads = jnp.dot(
         grads, grad_basis, precision=highest, preferred_element_type=jnp.float32
     )
-    rotated_grads = lax.psum(partial_grads, "wide")
+    devices = lax.axis_size("wide")
+    rotated_grads, far = (partial_grads, 1)
+    while far < devices:
+        rotated_grads = rotated_grads + lax.ppermute(
+            rotated_grads, "wide", [(i, i ^ far) for i in range(devices)]
+        )
+        far = 2 * far
     out_cols = rotated_grads.shape[1]
     running = jnp.zeros((rotated_acts.shape[1], out_cols), jnp.float32)
     for seq_label in range(SEQS):

time: 614 us -> 1240 us (2.02)
  waiting for transfers between devices: 351 us -> 913 us
  other arithmetic: 0.8 us -> 54.8 us
    ppermute x0 -> x4, waiting for transfers between devices: none -> 912 us  [per_device(): lax.ppermute(rotated_grads, 'wide', [(i, i ^ far) for i in range(devices)])]
    all_gather x1, waiting for transfers between devices: 160 us -> 0.01 us  [per_device(): lax.all_gather(activations, 'wide', axis=0, tiled=True)]
    psum x1, waiting for transfers between devices: 116 us -> 0.01 us  [per_device(): rotated_acts = lax.psum(partial_acts, 'narrow')]
    psum x1 -> x0, waiting for transfers between devices: 73.7 us -> none  [per_device(): rotated_grads = lax.psum(partial_grads, 'wide')]
    add x0 -> x4, other arithmetic: none -> 53.9 us  [per_device(): rotated_grads + lax.ppermute(rotated_grads, 'wide', [(i, i ^ far) for i i...]
  transfers between devices with their start and end apart: 3 -> 6, of which waited for: 3 -> 4; matrix products, arithmetic and copies ran while one was open for 25% -> 16% of each run, Pallas kernels for 0% -> 0%
where the time goes in v1:
time: 1240 us; the launch traced here: 1230 us
  waiting for transfers between devices  913 us (74%)
  matrix products  241 us (19%)
  other arithmetic  54.8 us (4%)
  between operations  16.5 us (1%)
    ppermute x4, waiting for transfers between devices, per_device(): lax.ppermute(rotated_grads, 'wide', [(i, i ^ far) for i in range(devices)])  912 us
    dot_general x1, matrix products, per_device(): jnp.dot(lax.all_gather(activations, 'wide', axis=0, tiled=True), act_basi...  128 us
    dot_general x4, matrix products, per_device(): jnp.dot(acts_window.T, grads_window, precision=highest, preferred_element...  95.1 us
    add x4, other arithmetic, per_device(): rotated_grads + lax.ppermute(rotated_grads, 'wide', [(i, i ^ far) for i i...  53.9 us
  transfers between devices with their start and end apart: 6, of which 4 were waited for; matrix products, arithmetic and copies ran while one was open for 16% of the time, Pallas kernels for 0%

profile of v1, /device:TPU:0, one launch (start us, length us, event | category | flops | bytes accessed | tf_op | source)
XLA Modules:
  0.0 1235.0 jit_solution(5611039043959261798)
XLA Ops:
  6.5 0.0 copy-start
  6.5 0.0 all-gather.2.cloned.1.call-start
  6.5 0.7 all-gather.2.cloned.1.call-update
  7.3 0.0 all-reduce.2.cloned.1.call-start
  7.3 1.2 copy-done
  8.5 18.1 %fusion.29 = f32[1024,2560]{1,0:T(8,128)S(1)} fusion(f32[1024,320]{0,1:T(8,128)} %param.7, f32[320,2560]{1,0:T(8,128)S(1)} %copy-done), kind=kOutput, calls=%fused_computation.41 | convolution fusion | flops 10066329600 | bytes 15073280 | tf_op jit(solution)/shard_map/dot_general | solution.py:30
  26.6 0.0 copy-start.2
  26.6 4.1 copy-done.2
  30.7 0.5 collective-permute-start
  31.2 18.3 %collective-permute-done = f32[1024,2560]{1,0:T(8,128)} collective-permute-done((f32[1024,2560]{1,0:T(8,128)S(1)}, f32[1024,2560]{1,0:T(8,128)}, u32[]{:S(2)}, u32[]{:S(2)}) %collective-permute-start) | collective-permute-done | bytes 10485792 | tf_op jit(solution)/shard_map/ppermute | solution.py:36
  49.5 13.7 %add.44 = f32[1024,2560]{1,0:T(8,128)} add(f32[1024,2560]{1,0:T(8,128)} %copy-done.2, f32[1024,2560]{1,0:T(8,128)} %collective-permute-done) | non-fusion elementwise | flops 2621440 | bytes 31457280 | tf_op jit(solution)/shard_map/add | solution.py:36
  63.2 2.2 collective-permute-start.1
  65.3 346.8 %collective-permute-done.1 = f32[1024,2560]{1,0:T(8,128)} collective-permute-done((f32[1024,2560]{1,0:T(8,128)}, f32[1024,2560]{1,0:T(8,128)}, u32[]{:S(2)}, u32[]{:S(2)}) %collective-permute-start.1) | collective-permute-done | bytes 10485792 | tf_op jit(solution)/shard_map/ppermute | solution.py:36
  412.1 13.3 %add.45 = f32[1024,2560]{1,0:T(8,128)} add(f32[1024,2560]{1,0:T(8,128)} %add.44, f32[1024,2560]{1,0:T(8,128)} %collective-permute-done.1) | non-fusion elementwise | flops 2621440 | bytes 31457280 | tf_op jit(solution)/shard_map/add | solution.py:36
  425.5 0.0 collective-permute-start.2
  425.5 227.7 %collective-permute-done.2 = f32[1024,2560]{1,0:T(8,128)} collective-permute-done((f32[1024,2560]{1,0:T(8,128)}, f32[1024,2560]{1,0:T(8,128)}, u32[]{:S(2)}, u32[]{:S(2)}) %collective-permute-start.2) | collective-permute-done | bytes 10485792 | tf_op jit(solution)/shard_map/ppermute | solution.py:36
  653.1 13.7 %add.46 = f32[1024,2560]{1,0:T(8,128)} add(f32[1024,2560]{1,0:T(8,128)} %add.45, f32[1024,2560]{1,0:T(8,128)} %collective-permute-done.2) | non-fusion elementwise | flops 2621440 | bytes 31457280 | tf_op jit(solution)/shard_map/add | solution.py:36
  666.9 0.0 copy-start.3
  666.9 2.0 collective-permute-start.3
  668.9 0.0 all-gather.2.cloned.1.call-done
  668.9 127.7 %fusion.28 = f32[1024,1088]{0,1:T(8,128)} fusion(f32[1024,8704]{1,0:T(8,128)} %all-gather.2.cloned.1.call-done, f32[8704,1088]{0,1:T(8,128)} %param.6), kind=kOutput, calls=%fused_computation.40 | convolution fusion | flops 116366770176 | bytes 77987840 | tf_op jit(solution)/shard_map/dot_general | solution.py:23
  796.5 0.0 all-reduce.2.cloned.1.call-update
  796.6 0.0 copy-done.3
  796.6 0.7 convert_reduce_fusion.3
  799.8 0.1 fusion.24
  799.9 319.4 %collective-permute-done.3 = f32[1024,2560]{1,0:T(8,128)} collective-permute-done((f32[1024,2560]{1,0:T(8,128)}, f32[1024,2560]{1,0:T(8,128)}, u32[]{:S(2)}, u32[]{:S(2)}) %collective-permute-start.3) | collective-permute-done | bytes 10485792 | tf_op jit(solution)/shard_map/ppermute | solution.py:36
  1119.3 13.2 %add.47 = f32[1024,2560]{1,0:T(8,128)} add(f32[1024,2560]{1,0:T(8,128)} %add.46, f32[1024,2560]{1,0:T(8,128)} %collective-permute-done.3) | non-fusion elementwise | flops 2621440 | bytes 31457280 | tf_op jit(solution)/shard_map/add | solution.py:36
  1132.4 0.0 all-reduce.2.cloned.1.call-done
  1132.4 0.0 slice-start
  1132.5 0.0 slice-start.3
  1132.5 0.0 slice-start.1
  1132.5 0.0 slice-start.2
  1132.5 0.0 slice-start.4
  1132.5 24.0 %convolution_multiply_fusion = f32[1088,2560]{1,0:T(8,128)} fusion(f32[1024,2560]{1,0:T(8,128)} %add.47, s32[]{:T(128)S(6)} %select_n.11, f32[512]{0:T(512)S(1)} %get-tuple-element.11, f32[1024,1088]{0,1:T(8,128)} %all-reduce.2.cloned.1.call-done), kind=kOutput, calls=%fused_computation | convolution fusion | flops 17116856320 | bytes 18615296 | tf_op jit(solution)/shard_map/dot_general | solution.py:44
  1156.5 0.0 slice-done
  1156.5 0.0 slice-done.3
  1156.5 0.0 slice-done.1
  1156.5 0.0 slice-done.2
  1156.5 0.0 slice-done.4
  1156.5 21.6 %convolution_multiply_fusion.1 = f32[1088,2560]{1,0:T(8,128)} fusion(f32[1024,2560]{1,0:T(8,128)S(1)} %bitcast.5, s32[]{:T(128)S(6)} %select_n.10, f32[512]{0:T(512)S(1)} %get-tuple-element.10, f32[1024,1088]{0,1:T(8,128)S(1)} %bitcast.7), kind=kOutput, calls=%fused_computation.1 | convolution fusion | flops 17116856320 | bytes 18615296 | tf_op jit(solution)/shard_map/dot_general | solution.py:44
  1178.2 21.5 %convolution_multiply_fusion.2 = f32[1088,2560]{1,0:T(8,128)} fusion(f32[1024,2560]{1,0:T(8,128)S(1)} %bitcast.5, s32[]{:T(128)S(6)} %select_n.9, f32[512]{0:T(512)S(1)} %get-tuple-element.12, f32[1024,1088]{0,1:T(8,128)S(1)} %bitcast.7), kind=kOutput, calls=%fused_computation.2 | convolution fusion | flops 17116856320 | bytes 18615296 | tf_op jit(solution)/shard_map/dot_general | solution.py:44
  1199.6 0.0 copy-start.1
  1199.6 28.0 %fusion.3 = f32[1088,2560]{1,0:T(8,128)} fusion(f32[1088,2560]{1,0:T(8,128)} %convolution_multiply_fusion, f32[1088,2560]{1,0:T(8,128)} %convolution_multiply_fusion.1, f32[1088,2560]{1,0:T(8,128)} %convolution_multiply_fusion.2, f32[1024,2560]{1,0:T(8,128)} %add.47, s32[]{:T(128)S(6)} %select_n.8, f32[512]{0:T(512)S(1)} %get-tuple-element.9, ...), kind=kOutput, calls=%fused_computation.7 | convolution fusion | flops 17127997440 | bytes 52038656 | tf_op jit(solution)/shard_map/dot_general | solution.py:44
  1227.6 0.0 copy-done.1
  (2 shorter events, 0.0 us)
Async XLA Ops:
  6.5 1.9 copy-start
  6.5 662.3 %all-gather.2.cloned.1.call-start = ((), (), s32[]{:S(2)}) async-start(), calls=%async_computation | async-start | bytes 37879808 | tf_op jit(solution)/shard_map/all_gather | solution.py:24
  7.3 1125.2 %all-reduce.2.cloned.1.call-start = ((), (), s32[]{:S(2)}) async-start(), calls=%async_computation.1 | async-start | bytes 8912896 | tf_op jit(solution)/shard_map/psum | solution.py:29
  26.6 4.1 copy-start.2
  30.7 18.8 %collective-permute-start = (f32[1024,2560]{1,0:T(8,128)S(1)}, f32[1024,2560]{1,0:T(8,128)}, u32[]{:S(2)}, u32[]{:S(2)}) collective-permute-start(f32[1024,2560]{1,0:T(8,128)S(1)} %fusion.29), channel_id=1, source_target_pairs={{0,2},{2,0},{4,6},{6,4},{8,10},{10,8},{12,14},{14,12},{16,18},{18,... | collective-permute-start | bytes 31457288 | tf_op jit(solution)/shard_map/ppermute | solution.py:36
  63.2 349.0 %collective-permute-start.1 = (f32[1024,2560]{1,0:T(8,128)}, f32[1024,2560]{1,0:T(8,128)}, u32[]{:S(2)}, u32[]{:S(2)}) collective-permute-start(f32[1024,2560]{1,0:T(8,128)} %add.44), channel_id=1, source_target_pairs={{0,4},{2,6},{4,0},{6,2},{8,12},{10,14},{12,8},{14,10},{16,20},{18,... | collective-permute-start | bytes 31457288 | tf_op jit(solution)/shard_map/ppermute | solution.py:36
  425.5 227.7 %collective-permute-start.2 = (f32[1024,2560]{1,0:T(8,128)}, f32[1024,2560]{1,0:T(8,128)}, u32[]{:S(2)}, u32[]{:S(2)}) collective-permute-start(f32[1024,2560]{1,0:T(8,128)} %add.45), channel_id=1, source_target_pairs={{0,8},{2,10},{4,12},{6,14},{8,0},{10,2},{12,4},{14,6},{16,24},{18,... | collective-permute-start | bytes 31457288 | tf_op jit(solution)/shard_map/ppermute | solution.py:36
  666.9 129.7 %copy-start.3 = (s32[1024]{0:T(1024)S(1)}, s32[1024]{0:T(1024)}, u32[]{:S(2)}) copy-start(s32[1024]{0:T(1024)} %param.9) | copy-start | bytes 12292
  666.9 452.4 %collective-permute-start.3 = (f32[1024,2560]{1,0:T(8,128)}, f32[1024,2560]{1,0:T(8,128)}, u32[]{:S(2)}, u32[]{:S(2)}) collective-permute-start(f32[1024,2560]{1,0:T(8,128)} %add.46), channel_id=1, source_target_pairs={{0,16},{2,18},{4,20},{6,22},{8,24},{10,26},{12,28},{14,30},{16,0},... | collective-permute-start | bytes 31457288 | tf_op jit(solution)/shard_map/ppermute | solution.py:36
  1132.4 24.0 %slice-start = ((s8[10485760]{0:T(1024)(128)(4,1)}), s8[4194304]{0:T(1024)(128)(4,1)S(1)}, s32[]{:S(2)}) async-start(s8[10485760]{0:T(1024)(128)(4,1)} %bitcast.4), calls=%async_computation.2 | async-start | bytes 8388608
  1132.5 24.0 %slice-start.3 = ((s8[4456448]{0:T(1024)(128)(4,1)}), s8[4194304]{0:T(1024)(128)(4,1)S(1)}, s32[]{:S(2)}) async-start(s8[4456448]{0:T(1024)(128)(4,1)} %bitcast.6), calls=%async_computation.5 | async-start | bytes 8388608
  1132.5 24.0 %slice-start.1 = ((s8[10485760]{0:T(1024)(128)(4,1)}), s8[4194304]{0:T(1024)(128)(4,1)S(1)}, s32[]{:S(2)}) async-start(s8[10485760]{0:T(1024)(128)(4,1)} %bitcast.4), calls=%async_computation.3 | async-start | bytes 8388608
  1132.5 24.0 %slice-start.2 = ((s8[10485760]{0:T(1024)(128)(4,1)}), s8[2097152]{0:T(1024)(128)(4,1)S(1)}, s32[]{:S(2)}) async-start(s8[10485760]{0:T(1024)(128)(4,1)} %bitcast.4), calls=%async_computation.4 | async-start | bytes 4194304
  1132.5 24.0 %slice-start.4 = ((s8[4456448]{0:T(1024)(128)(4,1)}), s8[262144]{0:T(1024)(128)(4,1)S(1)}, s32[]{:S(2)}) async-start(s8[4456448]{0:T(1024)(128)(4,1)} %bitcast.6), calls=%async_computation.6 | async-start | bytes 524288
  1199.6 28.0 %copy-start.1 = (f32[320,2560]{1,0:T(8,128)S(1)}, f32[320,2560]{1,0:T(8,128)}, u32[]{:S(2)}) copy-start(f32[320,2560]{1,0:T(8,128)} %param.8) | copy-start | bytes 9830404
Sparse Core Ops, SparseCore 0:
  8.9 300.9 all-gather.1
  796.7 111.9 all-reduce.1
